TPU v7x, 256 devices: a whole 4x4x8 slice. The times are simulated.
256 devices in a mesh: group: 8 (over z_lo, y), dev: 32 (over z_hi, x, core).
Axes of the slice: x: 4, y: 4, z: 8 (z_hi: 4, z_lo: 2; z = z_hi * 2 + z_lo), core: 2. Of those that a mesh axis runs over, the one named last changes fastest.
Arguments:
- right_side: float32 [3, 16, 64, 64, 128], P(None, 'group', 'dev'), may hold values from -60 to 60
- stiff_diag: float32 [3, 3, 16, 4096], P(None, None, 'group', 'dev'), may hold values from -0.1 to 12.75, as said below
- stiff_lower: float32 [3, 3, 13, 16, 4096], P(None, None, None, 'group', 'dev'), may hold values from -0.08 to 0.08
- fsai_diag: float32 [3, 3, 16, 4096], P(None, None, 'group', 'dev'), may hold values from -0.1 to 1, as said below
- fsai_lower: float32 [3, 3, 13, 16, 4096], P(None, None, None, 'group', 'dev'), may hold values from -0.12 to 0.12
- fsai_pattern: int32 [13, 16, 4096], P(None, 'group', 'dev'), may hold values 0 or 1
Outputs:
- solution: float32 [3, 16, 64, 64, 128], P(None, 'group', 'dev')
- residual: float32 [3, 16, 64, 64, 128], P(None, 'group', 'dev')
Inputs may be any that keep to these rules, and one draw needn't show every extreme that they name: `stiff_diag`: each 3 by 3 block is symmetric. `fsai_diag`: each 3 by 3 block is zero above its diagonal and positive on it.
All inputs are finite; a program needn't handle non-finite values. No bound on the sum of `fsai_pattern` on one device may be relied on, other than what follows from the above.
Results may differ from a plain program's by a relative error of at most 0.0003.
Values sent between devices are 32-bit elements; how exact they have to be, the bound alone decides.
A program may use at most 128 MiB of HBM per device.

v0:
```python
import jax
import jax.numpy as jnp
from jax import lax
from jax.sharding import PartitionSpec as P

ITERS = 2
highest = lax.Precision.HIGHEST
lower_offsets = [(0, 0, -1), (0, -1, -1), (0, -1, 0), (0, -1, 1)] + [
    (-1, row_step, column_step) for row_step in (-1, 0, 1) for column_step in (-1, 0, 1)
]


def with_halo(block, sides, width):
    for axis, dim in sides:
        count = lax.axis_size(axis)
        forward = [(i, i + 1) for i in range(count - 1)]
        backward = [(target, source) for source, target in forward]
        low = lax.ppermute(
            lax.slice_in_dim(block, block.shape[dim] - width, None, axis=dim), axis, forward
        )
        high = lax.ppermute(lax.slice_in_dim(block, 0, width, axis=dim), axis, backward)
        block = jnp.concatenate([low, block, high], axis=dim)
    return block


def from_behind(value, axis, steps):
    count = lax.axis_size(axis)
    first, last = (max(0, -steps), min(count, count - steps))
    return lax.ppermute(value, axis, [(source, source + steps) for source in range(first, last)])


def block_mul(coeffs, vector):
    return jnp.stack(
        [
            coeffs[target, 0][..., None] * vector[0]
            + coeffs[target, 1][..., None] * vector[1]
            + coeffs[target, 2][..., None] * vector[2]
            for target in range(3)
        ]
    )


def block_mul_transposed(coeffs, vector):
    return jnp.stack(
        [
            coeffs[0, target][..., None] * vector[0]
            + coeffs[1, target][..., None] * vector[1]
            + coeffs[2, target][..., None] * vector[2]
            for target in range(3)
        ]
    )


def pad_columns(vector):
    return jnp.pad(vector, ((0, 0), (0, 0), (0, 0), (1, 1), (0, 0)))


def local_gram(left_block, right_block):
    return jnp.einsum("azxyr,azxys->rs", left_block, right_block, precision=highest)


def combine(vector, coeffs):
    return jnp.einsum("azxyr,rs->azxys", vector, coeffs, precision=highest)


def gram_solve(matrix, right_terms):
    factor = jnp.linalg.cholesky(matrix)
    halfway = lax.linalg.triangular_solve(factor, right_terms, left_side=True, lower=True)
    return lax.linalg.triangular_solve(
        factor, halfway, left_side=True, lower=True, transpose_a=True
    )


def per_device(right_side, stiff_diag, stiff_lower, fsai_diag, fsai_lower, fsai_pattern):
    local_planes = right_side.shape[1]
    local_rows = right_side.shape[2]
    line_length = right_side.shape[3]
    slot_count = stiff_lower.shape[2]
    stiff_d = stiff_diag.reshape(3, 3, local_planes, local_rows, line_length)
    fsai_d = fsai_diag.reshape(3, 3, local_planes, local_rows, line_length)
    stiff_low = stiff_lower.reshape(3, 3, slot_count, local_planes, local_rows, line_length)
    kept = fsai_pattern.astype(jnp.float32)
    fsai_low = (fsai_lower * kept[None, None]).reshape(
        3, 3, slot_count, local_planes, local_rows, line_length
    )

    def lower_window(vector):
        rimmed = with_halo(vector, (("dev", 2),), 1)
        plane_under = from_behind(rimmed[:, local_planes - 1 :], "group", 1)
        return pad_columns(jnp.concatenate([plane_under, rimmed], axis=1))

    def gather_lower(diag_blocks, low_blocks, window_data, vector):
        result = block_mul(diag_blocks, vector)
        for slot_index, (depth_step, row_step, column_step) in enumerate(lower_offsets):
            picked = window_data[
                :,
                1 + depth_step : 1 + depth_step + local_planes,
                1 + row_step : 1 + row_step + local_rows,
                1 + column_step : 1 + column_step + line_length,
            ]
            result = result + block_mul(low_blocks[:, :, slot_index], picked)
        return result

    def push_upper(low_blocks, vector):
        buffer = None
        for slot_index, (depth_step, row_step, column_step) in enumerate(lower_offsets):
            slot_term = block_mul_transposed(low_blocks[:, :, slot_index], vector)
            placed = jnp.pad(
                slot_term,
                (
                    (0, 0),
                    (1 + depth_step, -depth_step),
                    (1 + row_step, 1 - row_step),
                    (1 + column_step, 1 - column_step),
                    (0, 0),
                ),
            )
            buffer = placed if buffer is None else buffer + placed
        inner_part = buffer[:, :, :, 1 : line_length + 1]
        rim_rows = jnp.concatenate(
            [inner_part[:, :, :1], inner_part[:, :, local_rows + 1 :]], axis=2
        )
        arrived = with_halo(rim_rows, (("dev", 2),), 1)
        core_part = inner_part[:, :, 1 : local_rows + 1]
        core_part = core_part.at[:, :, :1].add(arrived[:, :, :1])
        core_part = core_part.at[:, :, local_rows - 1 :].add(arrived[:, :, 3:])
        returned = from_behind(core_part[:, :1], "group", -1)
        return core_part[:, 1:].at[:, local_planes - 1 :].add(returned)

    def apply_fsai(vector):
        return gather_lower(fsai_d, fsai_low, lower_window(vector), vector)

    def apply_fsai_transposed(vector):
        diagonal_part = block_mul_transposed(fsai_d, vector)
        upper_sum = push_upper(fsai_low, vector)
        return diagonal_part + upper_sum

    def residual_sum(weighted):
        return lax.psum(local_gram(weighted, weighted), ("group", "dev"))

    solution = jnp.zeros_like(right_side)
    residual = right_side
    weighted = apply_fsai(residual)
    resid_gram = residual_sum(weighted)
    direction = apply_fsai_transposed(weighted)
    for iteration in range(ITERS):
        lower_sum = gather_lower(stiff_d, stiff_low, lower_window(direction), direction)
        apply_upper_sum = push_upper(stiff_low, direction)
        product = lower_sum + apply_upper_sum
        step_size = gram_solve(
            lax.psum(local_gram(direction, product), ("group", "dev")), resid_gram
        )
        solution = solution + combine(direction, step_size)
        residual = residual - combine(product, step_size)
        if iteration + 1 < ITERS:
            weighted = apply_fsai(residual)
            next_gram = residual_sum(weighted)
            precond = apply_fsai_transposed(weighted)
            conjugacy = gram_solve(resid_gram, next_gram)
            direction = precond + combine(direction, conjugacy)
            resid_gram = next_gram
    return (solution, residual)


def solution(mesh):
    return jax.shard_map(
        per_device,
        mesh=mesh,
        in_specs=(
            P(None, "group", "dev", None, None),
            P(None, None, "group", "dev"),
            P(None, None, None, "group", "dev"),
            P(None, None, "group", "dev"),
            P(None, None, None, "group", "dev"),
            P(None, "group", "dev"),
        ),
        out_specs=(P(None, "group", "dev", None, None), P(None, "group", "dev", None, None)),
        check_vma=False,
    )
```

profile of v0, /device:TPU:1, one launch (start us, length us, event | category | flops | bytes accessed | tf_op | source)
XLA Modules:
  0.0 1071.7 jit_solution(4820610917557618189)
XLA Ops:
  8.3 4.5 collective-permute-start
  12.8 1.9 collective-permute-start.1
  25.8 3.7 collective-permute-start.2
  31.3 5.2 collective-permute-done.2
  37.8 1.2 multiply_add_fusion.290
  39.0 1.2 multiply_add_fusion.289
  40.2 1.2 multiply_add_fusion.288
  41.4 1.2 multiply_add_fusion.296
  42.6 1.2 multiply_add_fusion.295
  63.6 1.4 fusion.48
  65.1 4.8 collective-permute-start.3
  71.4 1.9 collective-permute-start.4
  74.1 5.4 collective-permute-done.4
  79.6 1.3 collective-permute-start.5
  81.5 1.4 convolution_bitcast_fusion.5
  83.0 3.7 collective-permute-done.5
  87.0 3.9 collective-permute-start.6
  90.9 2.1 collective-permute-start.7
  102.7 1.4 fusion.36
  104.2 3.6 collective-permute-start.9
  107.8 1.9 collective-permute-start.10
  109.8 3.9 collective-permute-start.8
  114.2 1.6 collective-permute-done.10
  116.0 1.3 collective-permute-start.11
  117.3 4.0 collective-permute-done.8
  126.9 1.4 convolution_bitcast_fusion.6
  128.6 264.0 %all-reduce.65.cloned.1.call-done = (f32[128,128]{0,1:T(8,128)}, f32[128,128]{0,1:T(8,128)}) async-done(((f32[128,128]{0,1:T(8,128)}, f32[128,128]{0,1:T(8,128)}), (f32[128,128]{0,1:T(8,128)}, f32[128,128]{0,1:T(8,128)})) %all-reduce.65.cloned.1.call-update) | async-done | bytes 131088 | tf_op jit(solution)/shard_map/psum | solution.py:139
  394.4 11.7 %cholesky.59 = f32[128,128]{1,0:T(8,128)S(1)} custom-call(f32[128,128]{1,0:T(8,128)S(1)} %fusion.164), custom_call_target="Cholesky" | custom-call | tf_op jit(solution)/shard_map/jit(cholesky)/cholesky | solution.py:67
  407.5 9.8 custom-call.13
  420.2 4.9 collective-permute-start.12
  425.1 1.9 collective-permute-start.13
  427.0 11.7 %cholesky.70 = f32[128,128]{1,0:T(8,128)S(1)} custom-call(f32[128,128]{1,0:T(8,128)S(1)} %fusion.160), custom_call_target="Cholesky" | custom-call | tf_op jit(solution)/shard_map/jit(cholesky)/cholesky | solution.py:67
  440.4 1.8 collective-permute-start.14
  444.2 6.4 collective-permute-done.14
  450.8 1.2 multiply_add_fusion.125
  453.0 1.2 multiply_add_fusion.124
  454.2 1.2 multiply_add_fusion.123
  455.4 1.2 multiply_add_fusion.128
  457.7 1.2 multiply_add_fusion.127
  458.9 1.2 multiply_add_fusion.126
  461.2 1.2 multiply_add_fusion.131
  477.7 1.4 fusion.24
  480.0 3.3 collective-permute-start.15
  483.9 10.4 custom-call.15
  494.3 1.9 collective-permute-start.16
  496.3 1.4 convolution_bitcast_fusion.3
  498.8 3.8 collective-permute-done.16
  503.7 1.3 collective-permute-start.17
  505.0 238.5 %all-reduce.61.cloned.1.call-done = f32[128,128]{1,0:T(8,128)} async-done(((f32[128,128]{1,0:T(8,128)}), f32[128,128]{1,0:T(8,128)}) %all-reduce.61.cloned.1.call-update) | async-done | bytes 65552 | tf_op jit(solution)/shard_map/psum | solution.py:139
  756.5 2.5 collective-permute-start.18
  759.0 1.9 collective-permute-start.19
  762.6 1.4 fusion.12
  764.1 4.4 collective-permute-start.21
  768.5 1.9 collective-permute-start.22
  770.5 2.7 collective-permute-start.20
  773.6 2.9 collective-permute-done.22
  776.7 1.5 collective-permute-start.23
  778.2 1.8 collective-permute-done.20
  785.8 1.4 convolution_bitcast_fusion.1
  787.2 249.6 %all-reduce.63.cloned.1.call-done = f32[128,128]{0,1:T(8,128)} async-done(((f32[128,128]{0,1:T(8,128)}), f32[128,128]{0,1:T(8,128)}) %all-reduce.63.cloned.1.call-update) | async-done | bytes 65552 | tf_op jit(solution)/shard_map/psum | solution.py:151
  1038.6 11.7 %cholesky.81 = f32[128,128]{1,0:T(8,128)S(1)} custom-call(f32[128,128]{1,0:T(8,128)S(1)} %fusion.156), custom_call_target="Cholesky" | custom-call | tf_op jit(solution)/shard_map/jit(cholesky)/cholesky | solution.py:67
  1051.7 9.8 custom-call.17
  1062.5 1.2 convolution_subtract_fusion
  1063.7 1.2 convolution_add_fusion
  (769 shorter events, 106.5 us)
Async XLA Ops:
  7.2 385.4 %all-reduce.65.cloned.1.call-start = ((), (), s32[]{:S(2)}) async-start(), calls=%async_computation.2 | async-start | bytes 262144 | tf_op jit(solution)/shard_map/psum | solution.py:139
  8.3 17.4 %collective-permute-start = (f32[3,2,1,64,128]{4,3,2,1,0:T(8,128)S(1)}, f32[3,2,1,64,128]{4,3,2,1,0:T(8,128)S(1)}, u32[]{:S(2)}, u32[]{:S(2)}) collective-permute-start(f32[3,2,1,64,128]{4,3,2,1,0:T(8,128)S(1)} %get-tuple-element.502), channel_id=1, source_target_pairs={{0,1},{1,2},{2,3},{3,4},{4,5},{5,6},{6,7},{7,8},{8,9},{9,10},{10,1... | collective-permute-start | bytes 589832 | tf_op jit(solution)/shard_map/ppermute | solution.py:18
  12.8 13.0 %collective-permute-start.1 = (f32[3,2,1,64,128]{4,3,2,1,0:T(8,128)S(1)}, f32[3,2,1,64,128]{4,3,2,1,0:T(8,128)S(1)}, u32[]{:S(2)}, u32[]{:S(2)}) collective-permute-start(f32[3,2,1,64,128]{4,3,2,1,0:T(8,128)S(1)} %get-tuple-element.501), channel_id=1, source_target_pairs={{1,0},{2,1},{3,2},{4,3},{5,4},{6,5},{7,6},{8,7},{9,8},{10,9},{11,1... | collective-permute-start | bytes 589832 | tf_op jit(solution)/shard_map/ppermute | solution.py:21
  18.4 102.9 %copy-start.17 = (f32[2,2,64]{2,1,0:T(2,128)}, f32[2,2,64]{2,1,0:T(2,128)S(1)}, u32[]{:S(2)}) copy-start(f32[2,2,64]{2,1,0:T(2,128)S(1)} %get-tuple-element.651) | copy-start | bytes 3076
  18.4 103.0 %copy-start.19 = (f32[2,2,64]{2,1,0:T(2,128)}, f32[2,2,64]{2,1,0:T(2,128)S(1)}, u32[]{:S(2)}) copy-start(f32[2,2,64]{2,1,0:T(2,128)S(1)} %get-tuple-element.658) | copy-start | bytes 3076
  18.4 103.0 %copy-start.21 = (f32[2,2,64]{2,1,0:T(2,128)}, f32[2,2,64]{2,1,0:T(2,128)S(1)}, u32[]{:S(2)}) copy-start(f32[2,2,64]{2,1,0:T(2,128)S(1)} %get-tuple-element.659) | copy-start | bytes 3076
  18.4 103.4 %copy-start.11 = (f32[2,2,64]{2,1,0:T(2,128)}, f32[2,2,64]{2,1,0:T(2,128)S(1)}, u32[]{:S(2)}) copy-start(f32[2,2,64]{2,1,0:T(2,128)S(1)} %get-tuple-element.655) | copy-start | bytes 3076
  18.4 103.4 %copy-start.13 = (f32[2,2,64]{2,1,0:T(2,128)}, f32[2,2,64]{2,1,0:T(2,128)S(1)}, u32[]{:S(2)}) copy-start(f32[2,2,64]{2,1,0:T(2,128)S(1)} %get-tuple-element.656) | copy-start | bytes 3076
  18.5 103.4 %copy-start.15 = (f32[2,2,64]{2,1,0:T(2,128)}, f32[2,2,64]{2,1,0:T(2,128)S(1)}, u32[]{:S(2)}) copy-start(f32[2,2,64]{2,1,0:T(2,128)S(1)} %get-tuple-element.657) | copy-start | bytes 3076
  18.5 104.0 %copy-start.5 = (f32[2,2,64]{2,1,0:T(2,128)}, f32[2,2,64]{2,1,0:T(2,128)S(1)}, u32[]{:S(2)}) copy-start(f32[2,2,64]{2,1,0:T(2,128)S(1)} %get-tuple-element.652) | copy-start | bytes 3076
  18.5 104.0 %copy-start.7 = (f32[2,2,64]{2,1,0:T(2,128)}, f32[2,2,64]{2,1,0:T(2,128)S(1)}, u32[]{:S(2)}) copy-start(f32[2,2,64]{2,1,0:T(2,128)S(1)} %get-tuple-element.653) | copy-start | bytes 3076
  18.5 104.0 %copy-start.9 = (f32[2,2,64]{2,1,0:T(2,128)}, f32[2,2,64]{2,1,0:T(2,128)S(1)}, u32[]{:S(2)}) copy-start(f32[2,2,64]{2,1,0:T(2,128)S(1)} %get-tuple-element.654) | copy-start | bytes 3076
  19.2 42.9 %copy-start.130 = (f32[2,2,64]{2,1,0:T(2,128)}, f32[2,2,64]{2,1,0:T(2,128)S(1)}, u32[]{:S(2)}) copy-start(f32[2,2,64]{2,1,0:T(2,128)S(1)} %get-tuple-element.897) | copy-start | bytes 3076
  19.2 44.0 %copy-start.119 = (f32[2,2,64]{2,1,0:T(2,128)}, f32[2,2,64]{2,1,0:T(2,128)S(1)}, u32[]{:S(2)}) copy-start(f32[2,2,64]{2,1,0:T(2,128)S(1)} %get-tuple-element.896) | copy-start | bytes 3076
  19.2 44.0 %copy-start.122 = (f32[2,2,64]{2,1,0:T(2,128)}, f32[2,2,64]{2,1,0:T(2,128)S(1)}, u32[]{:S(2)}) copy-start(f32[2,2,64]{2,1,0:T(2,128)S(1)} %get-tuple-element.899) | copy-start | bytes 3076
  19.2 44.0 %copy-start.125 = (f32[2,2,64]{2,1,0:T(2,128)}, f32[2,2,64]{2,1,0:T(2,128)S(1)}, u32[]{:S(2)}) copy-start(f32[2,2,64]{2,1,0:T(2,128)S(1)} %get-tuple-element.902) | copy-start | bytes 3076
  19.8 43.4 %copy-start.134 = (f32[2,2,64]{2,1,0:T(2,128)}, f32[2,2,64]{2,1,0:T(2,128)S(1)}, u32[]{:S(2)}) copy-start(f32[2,2,64]{2,1,0:T(2,128)S(1)} %get-tuple-element.831) | copy-start | bytes 3076
  19.8 43.4 %copy-start.136 = (f32[2,2,64]{2,1,0:T(2,128)}, f32[2,2,64]{2,1,0:T(2,128)S(1)}, u32[]{:S(2)}) copy-start(f32[2,2,64]{2,1,0:T(2,128)S(1)} %get-tuple-element.833) | copy-start | bytes 3076
  19.8 43.4 %copy-start.138 = (f32[2,2,64]{2,1,0:T(2,128)}, f32[2,2,64]{2,1,0:T(2,128)S(1)}, u32[]{:S(2)}) copy-start(f32[2,2,64]{2,1,0:T(2,128)S(1)} %get-tuple-element.834) | copy-start | bytes 3076
  19.9 43.4 %copy-start.140 = (f32[2,2,64]{2,1,0:T(2,128)}, f32[2,2,64]{2,1,0:T(2,128)S(1)}, u32[]{:S(2)}) copy-start(f32[2,2,64]{2,1,0:T(2,128)S(1)} %get-tuple-element.836) | copy-start | bytes 3076
  19.9 43.4 %copy-start.142 = (f32[2,2,64]{2,1,0:T(2,128)}, f32[2,2,64]{2,1,0:T(2,128)S(1)}, u32[]{:S(2)}) copy-start(f32[2,2,64]{2,1,0:T(2,128)S(1)} %get-tuple-element.837) | copy-start | bytes 3076
  19.9 43.4 %copy-start.144 = (f32[2,2,64]{2,1,0:T(2,128)}, f32[2,2,64]{2,1,0:T(2,128)S(1)}, u32[]{:S(2)}) copy-start(f32[2,2,64]{2,1,0:T(2,128)S(1)} %get-tuple-element.839) | copy-start | bytes 3076
  23.2 101.7 %copy-start.47 = (f32[2,2,64]{2,1,0:T(2,128)}, f32[2,2,64]{2,1,0:T(2,128)S(1)}, u32[]{:S(2)}) copy-start(f32[2,2,64]{2,1,0:T(2,128)S(1)} %get-tuple-element.634) | copy-start | bytes 3076
  23.2 101.7 %copy-start.49 = (f32[2,2,64]{2,1,0:T(2,128)}, f32[2,2,64]{2,1,0:T(2,128)S(1)}, u32[]{:S(2)}) copy-start(f32[2,2,64]{2,1,0:T(2,128)S(1)} %get-tuple-element.635) | copy-start | bytes 3076
  23.2 101.7 %copy-start.51 = (f32[2,2,64]{2,1,0:T(2,128)}, f32[2,2,64]{2,1,0:T(2,128)S(1)}, u32[]{:S(2)}) copy-start(f32[2,2,64]{2,1,0:T(2,128)S(1)} %get-tuple-element.636) | copy-start | bytes 3076
  23.2 102.1 %copy-start.23 = (f32[2,2,64]{2,1,0:T(2,128)}, f32[2,2,64]{2,1,0:T(2,128)S(1)}, u32[]{:S(2)}) copy-start(f32[2,2,64]{2,1,0:T(2,128)S(1)} %get-tuple-element.633) | copy-start | bytes 3076
  23.2 102.1 %copy-start.25 = (f32[2,2,64]{2,1,0:T(2,128)}, f32[2,2,64]{2,1,0:T(2,128)S(1)}, u32[]{:S(2)}) copy-start(f32[2,2,64]{2,1,0:T(2,128)S(1)} %get-tuple-element.637) | copy-start | bytes 3076
  23.2 102.1 %copy-start.27 = (f32[2,2,64]{2,1,0:T(2,128)}, f32[2,2,64]{2,1,0:T(2,128)S(1)}, u32[]{:S(2)}) copy-start(f32[2,2,64]{2,1,0:T(2,128)S(1)} %get-tuple-element.638) | copy-start | bytes 3076
  23.2 102.1 %copy-start.29 = (f32[2,2,64]{2,1,0:T(2,128)}, f32[2,2,64]{2,1,0:T(2,128)S(1)}, u32[]{:S(2)}) copy-start(f32[2,2,64]{2,1,0:T(2,128)S(1)} %get-tuple-element.639) | copy-start | bytes 3076
  23.2 102.1 %copy-start.31 = (f32[2,2,64]{2,1,0:T(2,128)}, f32[2,2,64]{2,1,0:T(2,128)S(1)}, u32[]{:S(2)}) copy-start(f32[2,2,64]{2,1,0:T(2,128)S(1)} %get-tuple-element.640) | copy-start | bytes 3076
  23.2 102.1 %copy-start.33 = (f32[2,2,64]{2,1,0:T(2,128)}, f32[2,2,64]{2,1,0:T(2,128)S(1)}, u32[]{:S(2)}) copy-start(f32[2,2,64]{2,1,0:T(2,128)S(1)} %get-tuple-element.641) | copy-start | bytes 3076
  23.2 102.1 %copy-start.35 = (f32[2,2,64]{2,1,0:T(2,128)}, f32[2,2,64]{2,1,0:T(2,128)S(1)}, u32[]{:S(2)}) copy-start(f32[2,2,64]{2,1,0:T(2,128)S(1)} %get-tuple-element.851) | copy-start | bytes 3076
  23.2 102.1 %copy-start.37 = (f32[2,2,64]{2,1,0:T(2,128)}, f32[2,2,64]{2,1,0:T(2,128)S(1)}, u32[]{:S(2)}) copy-start(f32[2,2,64]{2,1,0:T(2,128)S(1)} %get-tuple-element.852) | copy-start | bytes 3076
  23.2 102.1 %copy-start.39 = (f32[2,2,64]{2,1,0:T(2,128)}, f32[2,2,64]{2,1,0:T(2,128)S(1)}, u32[]{:S(2)}) copy-start(f32[2,2,64]{2,1,0:T(2,128)S(1)} %get-tuple-element.853) | copy-start | bytes 3076
  23.2 102.1 %copy-start.41 = (f32[2,2,64]{2,1,0:T(2,128)}, f32[2,2,64]{2,1,0:T(2,128)S(1)}, u32[]{:S(2)}) copy-start(f32[2,2,64]{2,1,0:T(2,128)S(1)} %get-tuple-element.854) | copy-start | bytes 3076
  23.3 102.1 %copy-start.43 = (f32[2,2,64]{2,1,0:T(2,128)}, f32[2,2,64]{2,1,0:T(2,128)S(1)}, u32[]{:S(2)}) copy-start(f32[2,2,64]{2,1,0:T(2,128)S(1)} %get-tuple-element.855) | copy-start | bytes 3076
  23.3 102.1 %copy-start.45 = (f32[2,2,64]{2,1,0:T(2,128)}, f32[2,2,64]{2,1,0:T(2,128)S(1)}, u32[]{:S(2)}) copy-start(f32[2,2,64]{2,1,0:T(2,128)S(1)} %get-tuple-element.856) | copy-start | bytes 3076
  23.9 101.0 %copy-start.53 = (f32[2,2,64]{2,1,0:T(2,128)}, f32[2,2,64]{2,1,0:T(2,128)S(1)}, u32[]{:S(2)}) copy-start(f32[2,2,64]{2,1,0:T(2,128)S(1)} %get-tuple-element.615) | copy-start | bytes 3076
  25.8 10.7 collective-permute-start.2
  65.1 8.9 collective-permute-start.3
  71.4 8.0 collective-permute-start.4
  79.6 7.2 collective-permute-start.5
  87.0 14.7 %collective-permute-start.6 = (f32[3,2,1,64,128]{4,3,2,1,0:T(8,128)S(1)}, f32[3,2,1,64,128]{4,3,2,1,0:T(8,128)S(1)}, u32[]{:S(2)}, u32[]{:S(2)}) collective-permute-start(f32[3,2,1,64,128]{4,3,2,1,0:T(8,128)S(1)} %get-tuple-element.416), channel_id=1, source_target_pairs={{0,1},{1,2},{2,3},{3,4},{4,5},{5,6},{6,7},{7,8},{8,9},{9,10},{10,1... | collective-permute-start | bytes 589832 | tf_op jit(solution)/shard_map/ppermute | solution.py:18
  90.9 18.8 %collective-permute-start.7 = (f32[3,2,1,64,128]{4,3,2,1,0:T(8,128)S(1)}, f32[3,2,1,64,128]{4,3,2,1,0:T(8,128)S(1)}, u32[]{:S(2)}, u32[]{:S(2)}) collective-permute-start(f32[3,2,1,64,128]{4,3,2,1,0:T(8,128)S(1)} %get-tuple-element.417), channel_id=1, source_target_pairs={{1,0},{2,1},{3,2},{4,3},{5,4},{6,5},{7,6},{8,7},{9,8},{10,9},{11,1... | collective-permute-start | bytes 589832 | tf_op jit(solution)/shard_map/ppermute | solution.py:21
  104.2 10.0 collective-permute-start.9
  107.8 8.0 collective-permute-start.10
  109.8 11.5 %collective-permute-start.8 = (f32[3,1,4,64,128]{4,3,2,1,0:T(8,128)S(1)}, f32[3,1,4,64,128]{4,3,2,1,0:T(8,128)S(1)}, u32[]{:S(2)}, u32[]{:S(2)}) collective-permute-start(f32[3,1,4,64,128]{4,3,2,1,0:T(8,128)S(1)} %pad_maximum_fusion.5), channel_id=1, source_target_pairs={{0,32},{32,64},{64,96},{96,128},{128,160},{160,192},{192,224},{1,3... | collective-permute-start | bytes 1179656 | tf_op jit(solution)/shard_map/ppermute | solution.py:29
  116.0 10.2 collective-permute-start.11
  128.4 615.1 %all-reduce.61.cloned.1.call-start = ((), (), s32[]{:S(2)}) async-start(), calls=%async_computation | async-start | bytes 131072 | tf_op jit(solution)/shard_map/psum | solution.py:139
  420.2 20.2 %collective-permute-start.12 = (f32[3,2,1,64,128]{4,3,2,1,0:T(8,128)S(1)}, f32[3,2,1,64,128]{4,3,2,1,0:T(8,128)S(1)}, u32[]{:S(2)}, u32[]{:S(2)}) collective-permute-start(f32[3,2,1,64,128]{4,3,2,1,0:T(8,128)S(1)} %get-tuple-element.410), channel_id=1, source_target_pairs={{0,1},{1,2},{2,3},{3,4},{4,5},{5,6},{6,7},{7,8},{8,9},{9,10},{10,1... | collective-permute-start | bytes 589832 | tf_op jit(solution)/shard_map/ppermute | solution.py:18
  425.1 15.3 %collective-permute-start.13 = (f32[3,2,1,64,128]{4,3,2,1,0:T(8,128)S(1)}, f32[3,2,1,64,128]{4,3,2,1,0:T(8,128)S(1)}, u32[]{:S(2)}, u32[]{:S(2)}) collective-permute-start(f32[3,2,1,64,128]{4,3,2,1,0:T(8,128)S(1)} %get-tuple-element.411), channel_id=1, source_target_pairs={{1,0},{2,1},{3,2},{4,3},{5,4},{6,5},{7,6},{8,7},{9,8},{10,9},{11,1... | collective-permute-start | bytes 589832 | tf_op jit(solution)/shard_map/ppermute | solution.py:21
  440.4 10.2 collective-permute-start.14
  480.0 17.8 %collective-permute-start.15 = (f32[3,3,1,64,128]{4,3,2,1,0:T(8,128)}, f32[3,3,1,64,128]{4,3,2,1,0:T(8,128)}, u32[]{:S(2)}, u32[]{:S(2)}) collective-permute-start(f32[3,3,1,64,128]{4,3,2,1,0:T(8,128)} %get-tuple-element.166), channel_id=1, source_target_pairs={{0,1},{1,2},{2,3},{3,4},{4,5},{5,6},{6,7},{7,8},{8,9},{9,10},{10,1... | collective-permute-start | bytes 884744 | tf_op jit(solution)/shard_map/ppermute | solution.py:18
  494.3 8.3 collective-permute-start.16
  497.7 245.8 %copy-start.3 = (f32[1,128,128]{1,2,0:T(8,128)S(1)}, f32[1,128,128]{1,2,0:T(8,128)}, u32[]{:S(2)}) copy-start(f32[1,128,128]{1,2,0:T(8,128)} %custom-call.15) | copy-start | bytes 196612
  497.8 539.1 %all-reduce.63.cloned.1.call-start = ((), (), s32[]{:S(2)}) async-start(), calls=%async_computation.1 | async-start | bytes 131072 | tf_op jit(solution)/shard_map/psum | solution.py:151
  503.7 241.2 %collective-permute-start.17 = (f32[3,1,2,64,128]{4,3,2,1,0:T(8,128)S(1)}, f32[3,1,2,64,128]{4,3,2,1,0:T(8,128)S(1)}, u32[]{:S(2)}, u32[]{:S(2)}) collective-permute-start(f32[3,1,2,64,128]{4,3,2,1,0:T(8,128)S(1)} %slice.4621), channel_id=1, source_target_pairs={{32,0},{64,32},{96,64},{128,96},{160,128},{192,160},{224,192},{33,... | collective-permute-start | bytes 589832 | tf_op jit(solution)/shard_map/ppermute | solution.py:29
  756.5 5.1 collective-permute-start.18
  759.0 11.4 %collective-permute-start.19 = (f32[3,2,1,64,128]{4,3,2,1,0:T(8,128)S(1)}, f32[3,2,1,64,128]{4,3,2,1,0:T(8,128)S(1)}, u32[]{:S(2)}, u32[]{:S(2)}) collective-permute-start(f32[3,2,1,64,128]{4,3,2,1,0:T(8,128)S(1)} %get-tuple-element.325), channel_id=1, source_target_pairs={{1,0},{2,1},{3,2},{4,3},{5,4},{6,5},{7,6},{8,7},{9,8},{10,9},{11,1... | collective-permute-start | bytes 589832 | tf_op jit(solution)/shard_map/ppermute | solution.py:21
  764.1 9.5 collective-permute-start.21
  768.5 8.0 collective-permute-start.22
  770.5 9.5 collective-permute-start.20
  776.7 8.3 collective-permute-start.23
  785.8 275.7 %copy-start.2 = (f32[128,128]{1,0:T(8,128)S(1)}, f32[128,128]{1,0:T(8,128)}, u32[]{:S(2)}) copy-start(f32[128,128]{1,0:T(8,128)} %all-reduce.61.cloned.1.call-done) | copy-start | bytes 196612
  (243 other events, 1343.4 us)
Sparse Core Ops, SparseCore 0:
  128.5 264.0 all-reduce.64
  497.9 245.5 all-reduce.60
  787.4 249.4 all-reduce.62
where the time goes:
time: 1080 us; the launch traced here: 1070 us
  waiting for transfers between devices  788 us (73%)
  other arithmetic  168 us (16%)
  starting transfers between devices  65.3 us (6%)
  between operations  19.7 us (2%)
  local copies, waits for them, and re-layouts  17.9 us (2%)
  matrix products  12.7 us (1%)
    psum x2, waiting for transfers between devices, residual_sum(): return lax.psum(local_gram(weighted, weighted), ('group', 'dev'))  502 us
    psum x1, waiting for transfers between devices, per_device(): lax.psum(local_gram(direction, product), ('group', 'dev'))  250 us
    add x55, other arithmetic, block_mul(): coeffs[target, 0][..., None] * vector[0]  42.9 us
    add x50, other arithmetic, block_mul_transposed(): coeffs[0, target][..., None] * vector[0]  41.6 us
    another operation x9, other arithmetic, gram_solve(): factor = jnp.linalg.cholesky(matrix)  37.2 us
    ppermute x8, starting transfers between devices, with_halo(): lax.ppermute(lax.slice_in_dim(block, block.shape[dim] - width, None, axis...  32 us
    another operation x6, other arithmetic, gram_solve(): lax.linalg.triangular_solve(factor, halfway, left_side=True, lower=True,...  32 us
  transfers between devices with their start and end apart: 27, of which 13 were waited for; matrix products, arithmetic and copies ran while one was open for 7% of the time, Pallas kernels for 0%

commit v1 on v0

--- a/solution.py
+++ b/solution.py
@@ -136,7 +136,7 @@
         return diagonal_part + upper_sum
 
     def residual_sum(weighted):
-        return lax.psum(local_gram(weighted, weighted), ("group", "dev"))
+        return jnp.sum(lax.all_gather(local_gram(weighted, weighted), ("group", "dev")), axis=0)
 
     solution = jnp.zeros_like(right_side)
     residual = right_side

time: 1080 us -> 1630 us (1.51)
  waiting for transfers between devices: 788 us -> 1330 us
    all_gather x0 -> x2, waiting for transfers between devices: none -> 769 us  [residual_sum(): lax.all_gather(local_gram(weighted, weighted), ('group', 'dev'))]
    psum x2 -> x0, waiting for transfers between devices: 502 us -> none  [residual_sum(): return lax.psum(local_gram(weighted, weighted), ('group', 'dev'))]
    psum x1 -> x2, waiting for transfers between devices: 250 us -> 514 us  [per_device(): lax.psum(local_gram(direction, product), ('group', 'dev'))]
  transfers between devices with their start and end apart: 27 -> 28, of which waited for: 13 -> 14; matrix products, arithmetic and copies ran while one was open for 7% -> 6% of each run, Pallas kernels for 0% -> 0%
where the time goes in v1:
time: 1630 us
  waiting for transfers between devices  1330 us (82%)
  other arithmetic  173 us (11%)
  starting transfers between devices  77.8 us (5%)
  between operations  20.2 us (1%)
  local copies, waits for them, and re-layouts  17.3 us (1%)
    all_gather x2, waiting for transfers between devices, residual_sum(): lax.all_gather(local_gram(weighted, weighted), ('group', 'dev'))  769 us
    psum x2, waiting for transfers between devices, per_device(): lax.psum(local_gram(direction, product), ('group', 'dev'))  514 us
    ppermute x8, starting transfers between devices, with_halo(): lax.ppermute(lax.slice_in_dim(block, block.shape[dim] - width, None, axis...  42.1 us
    add x50, other arithmetic, block_mul_transposed(): coeffs[0, target][..., None] * vector[0]  40 us
    add x55, other arithmetic, block_mul(): coeffs[target, 0][..., None] * vector[0]  38.8 us
    another operation x9, other arithmetic, gram_solve(): factor = jnp.linalg.cholesky(matrix)  37.1 us
  transfers between devices with their start and end apart: 28, of which 14 were waited for; matrix products, arithmetic and copies ran while one was open for 6% of the time, Pallas kernels for 0%

profile of v1, /device:TPU:1, one launch (start us, length us, event | category | flops | bytes accessed | tf_op | source)
XLA Modules:
  0.0 1626.8 jit_solution(8350469601852302792)
XLA Ops:
  8.3 5.1 collective-permute-start.1
  13.4 1.9 collective-permute-start
  26.4 2.9 collective-permute-start.2
  31.1 6.8 collective-permute-done.2
  39.1 1.2 multiply_add_fusion.296
  40.3 1.2 multiply_add_fusion.295
  41.5 1.2 multiply_add_fusion.294
  42.7 1.2 multiply_add_fusion.290
  64.4 1.4 fusion.48
  65.9 3.2 collective-permute-start.3
  70.5 1.9 collective-permute-start.4
  72.8 5.8 collective-permute-done.4
  78.7 1.3 collective-permute-start.5
  80.2 5.6 collective-permute-done.5
  86.2 3.6 collective-permute-start.6
  89.8 2.4 collective-permute-start.7
  100.7 1.4 fusion.36
  102.2 3.6 collective-permute-start.9
  105.9 3.9 collective-permute-start.8
  109.9 1.9 collective-permute-start.10
  112.3 5.6 collective-permute-done.10
  118.0 1.5 collective-permute-start.11
  125.3 1.4 convolution_bitcast_fusion.6
  126.8 1.4 convolution_bitcast_fusion.5
  128.5 260.4 %all-reduce.59.cloned.1.call-done = f32[128,128]{0,1:T(8,128)} async-done(((f32[128,128]{0,1:T(8,128)}), f32[128,128]{0,1:T(8,128)}) %all-reduce.59.cloned.1.call-update) | async-done | bytes 65552 | tf_op jit(solution)/shard_map/psum | solution.py:151
  390.7 11.7 cholesky.59
  403.7 9.8 custom-call.13
  413.5 401.2 %all-gather.5.cloned.1.call-done = f32[32768,128]{1,0:T(8,128)} async-done(((f32[128,128]{1,0:T(8,128)}), f32[32768,128]{1,0:T(8,128)}) %all-gather.5.cloned.1.call-update) | async-done | bytes 16777232 | tf_op jit(solution)/shard_map/all_gather | solution.py:139
  814.7 6.6 reduce_sum.18
  822.4 3.9 collective-permute-start.12
  826.4 2.4 collective-permute-start.13
  829.2 4.2 collective-permute-done.13
  833.4 2.0 collective-permute-start.14
  837.4 3.4 collective-permute-done.14
  844.1 1.2 multiply_add_fusion.128
  845.3 1.2 multiply_add_fusion.127
  846.5 1.2 multiply_add_fusion.126
  847.9 1.2 multiply_add_fusion.131
  849.2 1.2 multiply_add_fusion.125
  851.7 1.2 multiply_add_fusion.123
  853.5 1.4 convolution_bitcast_fusion.3
  868.9 1.4 fusion.24
  871.2 15.8 collective-permute-start.15
  887.1 11.7 cholesky.70
  898.9 1.9 collective-permute-start.16
  901.5 6.3 collective-permute-done.16
  907.9 1.3 collective-permute-start.17
  909.8 9.8 custom-call.15
  919.7 367.5 %all-gather.7.cloned.1.call-done = f32[32768,128]{1,0:T(8,128)} async-done(((f32[128,128]{1,0:T(8,128)}), f32[32768,128]{1,0:T(8,128)}) %all-gather.7.cloned.1.call-update) | async-done | bytes 16777232 | tf_op jit(solution)/shard_map/all_gather | solution.py:139
  1287.1 6.6 reduce_sum.19
  1305.0 5.6 collective-permute-start.18
  1310.7 1.9 collective-permute-start.19
  1313.6 1.4 fusion.12
  1315.1 4.4 collective-permute-start.21
  1319.6 1.3 collective-permute-start.20
  1320.9 1.9 collective-permute-start.22
  1323.2 5.7 collective-permute-done.22
  1329.1 1.5 collective-permute-start.23
  1336.5 1.4 convolution_bitcast_fusion.1
  1337.9 254.0 %all-reduce.61.cloned.1.call-done = f32[128,128]{0,1:T(8,128)} async-done(((f32[128,128]{0,1:T(8,128)}), f32[128,128]{0,1:T(8,128)}) %all-reduce.61.cloned.1.call-update) | async-done | bytes 65552 | tf_op jit(solution)/shard_map/psum | solution.py:151
  1593.7 11.7 cholesky.81
  1606.8 9.8 custom-call.17
  1617.1 1.2 convolution_subtract_fusion
  1618.8 1.2 convolution_add_fusion
  (834 shorter events, 99.0 us)
Async XLA Ops:
  7.2 381.7 %all-reduce.59.cloned.1.call-start = ((), (), s32[]{:S(2)}) async-start(), calls=%async_computation | async-start | bytes 131072 | tf_op jit(solution)/shard_map/psum | solution.py:151
  8.3 18.1 %collective-permute-start.1 = (f32[3,2,1,64,128]{4,3,2,1,0:T(8,128)S(1)}, f32[3,2,1,64,128]{4,3,2,1,0:T(8,128)S(1)}, u32[]{:S(2)}, u32[]{:S(2)}) collective-permute-start(f32[3,2,1,64,128]{4,3,2,1,0:T(8,128)S(1)} %get-tuple-element.499), channel_id=1, source_target_pairs={{1,0},{2,1},{3,2},{4,3},{5,4},{6,5},{7,6},{8,7},{9,8},{10,9},{11,1... | collective-permute-start | bytes 589832 | tf_op jit(solution)/shard_map/ppermute | solution.py:21
  13.4 12.9 collective-permute-start
  19.0 40.0 %copy-start.148 = (f32[2,2,64]{2,1,0:T(2,128)}, f32[2,2,64]{2,1,0:T(2,128)S(1)}, u32[]{:S(2)}) copy-start(f32[2,2,64]{2,1,0:T(2,128)S(1)} %get-tuple-element.658) | copy-start | bytes 3076
  19.0 40.0 %copy-start.150 = (f32[2,2,64]{2,1,0:T(2,128)}, f32[2,2,64]{2,1,0:T(2,128)S(1)}, u32[]{:S(2)}) copy-start(f32[2,2,64]{2,1,0:T(2,128)S(1)} %get-tuple-element.659) | copy-start | bytes 3076
  19.0 40.0 %copy-start.152 = (f32[2,2,64]{2,1,0:T(2,128)}, f32[2,2,64]{2,1,0:T(2,128)S(1)}, u32[]{:S(2)}) copy-start(f32[2,2,64]{2,1,0:T(2,128)S(1)} %get-tuple-element.660) | copy-start | bytes 3076
  19.1 40.0 %copy-start.154 = (f32[2,2,64]{2,1,0:T(2,128)}, f32[2,2,64]{2,1,0:T(2,128)S(1)}, u32[]{:S(2)}) copy-start(f32[2,2,64]{2,1,0:T(2,128)S(1)} %get-tuple-element.661) | copy-start | bytes 3076
  19.1 40.0 %copy-start.156 = (f32[2,2,64]{2,1,0:T(2,128)}, f32[2,2,64]{2,1,0:T(2,128)S(1)}, u32[]{:S(2)}) copy-start(f32[2,2,64]{2,1,0:T(2,128)S(1)} %get-tuple-element.662) | copy-start | bytes 3076
  19.1 40.0 %copy-start.158 = (f32[2,2,64]{2,1,0:T(2,128)}, f32[2,2,64]{2,1,0:T(2,128)S(1)}, u32[]{:S(2)}) copy-start(f32[2,2,64]{2,1,0:T(2,128)S(1)} %get-tuple-element.663) | copy-start | bytes 3076
  19.1 40.0 %copy-start.160 = (f32[2,2,64]{2,1,0:T(2,128)}, f32[2,2,64]{2,1,0:T(2,128)S(1)}, u32[]{:S(2)}) copy-start(f32[2,2,64]{2,1,0:T(2,128)S(1)} %get-tuple-element.664) | copy-start | bytes 3076
  19.1 40.0 %copy-start.162 = (f32[2,2,64]{2,1,0:T(2,128)}, f32[2,2,64]{2,1,0:T(2,128)S(1)}, u32[]{:S(2)}) copy-start(f32[2,2,64]{2,1,0:T(2,128)S(1)} %get-tuple-element.665) | copy-start | bytes 3076
  19.1 40.0 %copy-start.164 = (f32[2,2,64]{2,1,0:T(2,128)}, f32[2,2,64]{2,1,0:T(2,128)S(1)}, u32[]{:S(2)}) copy-start(f32[2,2,64]{2,1,0:T(2,128)S(1)} %get-tuple-element.666) | copy-start | bytes 3076
  19.7 34.9 %copy-start.196 = (f32[2,2,64]{2,1,0:T(2,128)}, f32[2,2,64]{2,1,0:T(2,128)S(1)}, u32[]{:S(2)}) copy-start(f32[2,2,64]{2,1,0:T(2,128)S(1)} %get-tuple-element.751) | copy-start | bytes 3076
  19.7 34.9 %copy-start.198 = (f32[2,2,64]{2,1,0:T(2,128)}, f32[2,2,64]{2,1,0:T(2,128)S(1)}, u32[]{:S(2)}) copy-start(f32[2,2,64]{2,1,0:T(2,128)S(1)} %get-tuple-element.752) | copy-start | bytes 3076
  19.7 34.9 %copy-start.200 = (f32[2,2,64]{2,1,0:T(2,128)}, f32[2,2,64]{2,1,0:T(2,128)S(1)}, u32[]{:S(2)}) copy-start(f32[2,2,64]{2,1,0:T(2,128)S(1)} %get-tuple-element.753) | copy-start | bytes 3076
  19.7 42.0 %copy-start.136 = (f32[2,2,64]{2,1,0:T(2,128)}, f32[2,2,64]{2,1,0:T(2,128)S(1)}, u32[]{:S(2)}) copy-start(f32[2,2,64]{2,1,0:T(2,128)S(1)} %get-tuple-element.894) | copy-start | bytes 3076
  19.8 42.0 %copy-start.138 = (f32[2,2,64]{2,1,0:T(2,128)}, f32[2,2,64]{2,1,0:T(2,128)S(1)}, u32[]{:S(2)}) copy-start(f32[2,2,64]{2,1,0:T(2,128)S(1)} %get-tuple-element.897) | copy-start | bytes 3076
  19.8 42.0 %copy-start.140 = (f32[2,2,64]{2,1,0:T(2,128)}, f32[2,2,64]{2,1,0:T(2,128)S(1)}, u32[]{:S(2)}) copy-start(f32[2,2,64]{2,1,0:T(2,128)S(1)} %get-tuple-element.900) | copy-start | bytes 3076
  19.8 43.1 %copy-start.112 = (f32[2,2,64]{2,1,0:T(2,128)}, f32[2,2,64]{2,1,0:T(2,128)S(1)}, u32[]{:S(2)}) copy-start(f32[2,2,64]{2,1,0:T(2,128)S(1)} %get-tuple-element.892) | copy-start | bytes 3076
  19.8 43.1 %copy-start.114 = (f32[2,2,64]{2,1,0:T(2,128)}, f32[2,2,64]{2,1,0:T(2,128)S(1)}, u32[]{:S(2)}) copy-start(f32[2,2,64]{2,1,0:T(2,128)S(1)} %get-tuple-element.895) | copy-start | bytes 3076
  19.8 43.1 %copy-start.116 = (f32[2,2,64]{2,1,0:T(2,128)}, f32[2,2,64]{2,1,0:T(2,128)S(1)}, u32[]{:S(2)}) copy-start(f32[2,2,64]{2,1,0:T(2,128)S(1)} %get-tuple-element.898) | copy-start | bytes 3076
  19.8 44.1 %copy-start.106 = (f32[2,2,64]{2,1,0:T(2,128)}, f32[2,2,64]{2,1,0:T(2,128)S(1)}, u32[]{:S(2)}) copy-start(f32[2,2,64]{2,1,0:T(2,128)S(1)} %get-tuple-element.893) | copy-start | bytes 3076
  19.8 44.1 %copy-start.108 = (f32[2,2,64]{2,1,0:T(2,128)}, f32[2,2,64]{2,1,0:T(2,128)S(1)}, u32[]{:S(2)}) copy-start(f32[2,2,64]{2,1,0:T(2,128)S(1)} %get-tuple-element.896) | copy-start | bytes 3076
  19.8 44.1 %copy-start.110 = (f32[2,2,64]{2,1,0:T(2,128)}, f32[2,2,64]{2,1,0:T(2,128)S(1)}, u32[]{:S(2)}) copy-start(f32[2,2,64]{2,1,0:T(2,128)S(1)} %get-tuple-element.899) | copy-start | bytes 3076
  20.5 40.1 %copy-start.166 = (f32[2,2,64]{2,1,0:T(2,128)}, f32[2,2,64]{2,1,0:T(2,128)S(1)}, u32[]{:S(2)}) copy-start(f32[2,2,64]{2,1,0:T(2,128)S(1)} %get-tuple-element.795) | copy-start | bytes 3076
  20.5 40.1 %copy-start.168 = (f32[2,2,64]{2,1,0:T(2,128)}, f32[2,2,64]{2,1,0:T(2,128)S(1)}, u32[]{:S(2)}) copy-start(f32[2,2,64]{2,1,0:T(2,128)S(1)} %get-tuple-element.796) | copy-start | bytes 3076
  20.5 40.1 %copy-start.170 = (f32[2,2,64]{2,1,0:T(2,128)}, f32[2,2,64]{2,1,0:T(2,128)S(1)}, u32[]{:S(2)}) copy-start(f32[2,2,64]{2,1,0:T(2,128)S(1)} %get-tuple-element.797) | copy-start | bytes 3076
  20.5 40.1 %copy-start.172 = (f32[2,2,64]{2,1,0:T(2,128)}, f32[2,2,64]{2,1,0:T(2,128)S(1)}, u32[]{:S(2)}) copy-start(f32[2,2,64]{2,1,0:T(2,128)S(1)} %get-tuple-element.798) | copy-start | bytes 3076
  20.5 40.1 %copy-start.174 = (f32[2,2,64]{2,1,0:T(2,128)}, f32[2,2,64]{2,1,0:T(2,128)S(1)}, u32[]{:S(2)}) copy-start(f32[2,2,64]{2,1,0:T(2,128)S(1)} %get-tuple-element.799) | copy-start | bytes 3076
  20.5 40.1 %copy-start.176 = (f32[2,2,64]{2,1,0:T(2,128)}, f32[2,2,64]{2,1,0:T(2,128)S(1)}, u32[]{:S(2)}) copy-start(f32[2,2,64]{2,1,0:T(2,128)S(1)} %get-tuple-element.800) | copy-start | bytes 3076
  23.2 40.8 %copy-start.178 = (f32[2,2,64]{2,1,0:T(2,128)}, f32[2,2,64]{2,1,0:T(2,128)S(1)}, u32[]{:S(2)}) copy-start(f32[2,2,64]{2,1,0:T(2,128)S(1)} %get-tuple-element.758) | copy-start | bytes 3076
  23.2 40.8 %copy-start.180 = (f32[2,2,64]{2,1,0:T(2,128)}, f32[2,2,64]{2,1,0:T(2,128)S(1)}, u32[]{:S(2)}) copy-start(f32[2,2,64]{2,1,0:T(2,128)S(1)} %get-tuple-element.759) | copy-start | bytes 3076
  23.2 40.8 %copy-start.182 = (f32[2,2,64]{2,1,0:T(2,128)}, f32[2,2,64]{2,1,0:T(2,128)S(1)}, u32[]{:S(2)}) copy-start(f32[2,2,64]{2,1,0:T(2,128)S(1)} %get-tuple-element.761) | copy-start | bytes 3076
  23.2 40.8 %copy-start.184 = (f32[2,2,64]{2,1,0:T(2,128)}, f32[2,2,64]{2,1,0:T(2,128)S(1)}, u32[]{:S(2)}) copy-start(f32[2,2,64]{2,1,0:T(2,128)S(1)} %get-tuple-element.762) | copy-start | bytes 3076
  23.2 40.8 %copy-start.186 = (f32[2,2,64]{2,1,0:T(2,128)}, f32[2,2,64]{2,1,0:T(2,128)S(1)}, u32[]{:S(2)}) copy-start(f32[2,2,64]{2,1,0:T(2,128)S(1)} %get-tuple-element.764) | copy-start | bytes 3076
  23.2 40.8 %copy-start.188 = (f32[2,2,64]{2,1,0:T(2,128)}, f32[2,2,64]{2,1,0:T(2,128)S(1)}, u32[]{:S(2)}) copy-start(f32[2,2,64]{2,1,0:T(2,128)S(1)} %get-tuple-element.765) | copy-start | bytes 3076
  23.9 98.9 %copy-start.4 = (f32[2,2,64]{2,1,0:T(2,128)}, f32[2,2,64]{2,1,0:T(2,128)S(1)}, u32[]{:S(2)}) copy-start(f32[2,2,64]{2,1,0:T(2,128)S(1)} %get-tuple-element.550) | copy-start | bytes 3076
  23.9 98.9 %copy-start.6 = (f32[2,2,64]{2,1,0:T(2,128)}, f32[2,2,64]{2,1,0:T(2,128)S(1)}, u32[]{:S(2)}) copy-start(f32[2,2,64]{2,1,0:T(2,128)S(1)} %get-tuple-element.557) | copy-start | bytes 3076
  23.9 99.4 %copy-start.2 = (f32[2,2,64]{2,1,0:T(2,128)}, f32[2,2,64]{2,1,0:T(2,128)S(1)}, u32[]{:S(2)}) copy-start(f32[2,2,64]{2,1,0:T(2,128)S(1)} %get-tuple-element.556) | copy-start | bytes 3076
  26.4 11.5 collective-permute-start.2
  65.9 6.8 collective-permute-start.3
  70.5 8.0 collective-permute-start.4
  78.7 7.2 collective-permute-start.5
  86.2 14.2 collective-permute-start.6
  89.8 16.1 collective-permute-start.7
  102.2 10.0 collective-permute-start.9
  105.9 13.6 collective-permute-start.8
  109.9 8.0 collective-permute-start.10
  118.0 6.5 collective-permute-start.11
  126.7 688.0 %all-gather.5.cloned.1.call-start = ((), (), s32[]{:S(2)}) async-start(), calls=%async_computation.2 | async-start | bytes 16842752 | tf_op jit(solution)/shard_map/all_gather | solution.py:139
  128.2 1158.9 %all-gather.7.cloned.1.call-start = ((), (), s32[]{:S(2)}) async-start(), calls=%async_computation.3 | async-start | bytes 16842752 | tf_op jit(solution)/shard_map/all_gather | solution.py:139
  822.4 6.7 collective-permute-start.12
  826.4 7.0 collective-permute-start.13
  833.4 7.4 collective-permute-start.14
  855.0 737.0 %all-reduce.61.cloned.1.call-start = ((), (), s32[]{:S(2)}) async-start(), calls=%async_computation.1 | async-start | bytes 131072 | tf_op jit(solution)/shard_map/psum | solution.py:151
  871.2 30.2 %collective-permute-start.15 = (f32[3,3,1,64,128]{4,3,2,1,0:T(8,128)}, f32[3,3,1,64,128]{4,3,2,1,0:T(8,128)S(1)}, u32[]{:S(2)}, u32[]{:S(2)}) collective-permute-start(f32[3,3,1,64,128]{4,3,2,1,0:T(8,128)} %get-tuple-element.164), channel_id=1, source_target_pairs={{0,1},{1,2},{2,3},{3,4},{4,5},{5,6},{6,7},{7,8},{8,9},{9,10},{10,1... | collective-permute-start | bytes 884744 | tf_op jit(solution)/shard_map/ppermute | solution.py:18
  898.9 8.9 collective-permute-start.16
  907.9 11.7 collective-permute-start.17
  1305.0 8.2 collective-permute-start.18
  1310.7 8.9 collective-permute-start.19
  1315.1 8.0 collective-permute-start.21
  1319.6 11.0 collective-permute-start.20
  1320.9 8.0 collective-permute-start.22
  1329.1 6.7 collective-permute-start.23
  (274 other events, 1473.2 us)
Sparse Core Ops, SparseCore 0:
  126.9 261.9 all-reduce.58
  391.3 423.3 all-gather.4
  855.1 431.9 all-gather.6
  1338.0 253.8 all-reduce.60
